TPU v7x, 32 devices: a whole 2x2x4 slice. The times are simulated.
32 devices in a mesh: dp: 16 (over z, y, core), mp: 2 (over x).
Axes of the slice: x: 2, y: 2, z: 4, core: 2. Of those that a mesh axis runs over, the one named last changes fastest.
Arguments:
- tokens: bfloat16 [2048, 2048], P(('dp', 'mp')), may hold values from -6 to 6
- lengths: int32 [22], replicated, may hold values from 1 to 1024, 2048 in all
- w_in: bfloat16 [2048, 2048], P('dp'), may hold values from -0.125 to 0.125
- w_forget: bfloat16 [2048, 2048], P('dp'), may hold values from -0.125 to 0.125
- w_gate: bfloat16 [2048, 2048], P('dp'), may hold values from -0.125 to 0.125
- w_out: bfloat16 [2048, 2048], P('dp'), may hold values from -0.125 to 0.125
- attn_gain: bfloat16 [2048], P('dp'), may hold values from 0.5 to 1.5
- mix_gain: bfloat16 [2048], P('dp'), may hold values from 0.5 to 1.5
- bound_table: bfloat16 [24, 2048], P(None, 'dp'), may hold values from -14 to 3
- ff_gate: bfloat16 [2048, 5632], P('dp', 'mp'), may hold values from -0.125 to 0.125
- ff_up: bfloat16 [2048, 5632], P('dp', 'mp'), may hold values from -0.125 to 0.125
- ff_down: bfloat16 [5632, 2048], P('mp', 'dp'), may hold values from -0.078125 to 0.078125
- mlp_gain: bfloat16 [2048], P('dp'), may hold values from 0.5 to 1.5
- out_grad: bfloat16 [2048, 2048], P(('dp', 'mp')), may hold values from -6 to 6
Outputs:
- result: bfloat16 [2048, 2048], P(('dp', 'mp'))
- token_grad: float32 [2048, 2048], P(('dp', 'mp'))
- grad_w_in: float32 [2048, 2048], P('dp')
- grad_w_forget: float32 [2048, 2048], P('dp')
- grad_w_gate: float32 [2048, 2048], P('dp')
- grad_w_out: float32 [2048, 2048], P('dp')
- grad_attn_gain: float32 [2048], P('dp')
- grad_mix_gain: float32 [2048], P('dp')
- grad_bound_table: float32 [24, 2048], P(None, 'dp')
- grad_ff_gate: float32 [2048, 5632], P('dp', 'mp')
- grad_ff_up: float32 [2048, 5632], P('dp', 'mp')
- grad_ff_down: float32 [5632, 2048], P('mp', 'dp')
- grad_mlp_gain: float32 [2048], P('dp')
Inputs may be any that keep to these rules, and one draw needn't show every extreme that they name: lengths of 22 sequences packed end to end; they sum to 2048 and the longest is 1024.
All inputs are finite; a program needn't handle non-finite values.
Results may differ from a plain program's by a relative error of at most 0.0085.
Values may be sent and summed in bfloat16 or wider, within the bound.
No kernel may reach another device: no remote copies, remote signals or barrier semaphores. Data moves between devices by JAX's collectives and lax.ppermute only.
A program may use at most 384 MiB of HBM per device.

v0:
```python
import jax
import jax.numpy as jnp
from jax import lax
from jax.sharding import PartitionSpec as P

LAYER = 12
epsilon = 1e-06


def entering(value, axis, join, neutral, backward):
    count, mine = (lax.axis_size(axis), lax.axis_index(axis))
    pieces = jax.tree.map(lambda part: lax.all_gather(part, axis), value)
    if backward:
        pieces = jax.tree.map(lambda part: part[::-1], pieces)
        mine = count - 1 - mine
    running = jax.tree.map(
        lambda part, zero: jnp.full_like(part, 0) + jnp.asarray(zero, part.dtype), value, neutral
    )

    def turn(position, running):
        longer = join(running, jax.tree.map(lambda part: part[position], pieces))
        return jax.tree.map(lambda new, old: jnp.where(position < mine, new, old), longer, running)

    return lax.fori_loop(0, count - 1, turn, running)


def contract_rows(left, right):
    return lax.dot_general(
        left, right, (((0,), (0,)), ((), ())), preferred_element_type=jnp.float32
    )


def times_transposed(left, right):
    return lax.dot_general(
        left, right, (((1,), (1,)), ((), ())), preferred_element_type=jnp.float32
    )


def combine(earlier, later):
    return (earlier[0] * later[0], later[0] * earlier[1] + later[1])


def inverse_rms(value):
    return lax.rsqrt(jnp.mean(value * value, axis=-1, keepdims=True) + epsilon)


def sigmoid_slope(raw, sig):
    return sig * (1.0 + raw * (1.0 - sig))


def per_device(
    tokens,
    lengths,
    w_in,
    w_forget,
    w_gate,
    w_out,
    attn_gain,
    mix_gain,
    bound_table,
    ff_gate,
    ff_up,
    ff_down,
    mlp_gain,
    out_grad,
):
    whole = lax.all_gather(tokens, "mp", axis=0, tiled=True)
    mixer = (
        lax.all_gather(w_in, "dp", axis=0, tiled=True),
        lax.all_gather(w_forget, "dp", axis=0, tiled=True),
        lax.all_gather(w_gate, "dp", axis=0, tiled=True),
        lax.all_gather(w_out, "dp", axis=0, tiled=True),
        lax.all_gather(attn_gain, "dp", axis=0, tiled=True),
        lax.all_gather(mix_gain, "dp", axis=0, tiled=True),
        lax.all_gather(bound_table, "dp", axis=1, tiled=True),
    )
    dense = (
        lax.all_gather(ff_gate, "dp", axis=0, tiled=True),
        lax.all_gather(ff_up, "dp", axis=0, tiled=True),
        lax.all_gather(ff_down, "dp", axis=1, tiled=True),
        lax.all_gather(mlp_gain, "dp", axis=0, tiled=True),
    )
    row_count = whole.shape[0]
    half_rows = row_count // lax.axis_size("mp")
    width = whole.shape[1]
    layer_rows = bound_table.shape[0]
    mp_index = lax.axis_index("mp")
    starts = jnp.cumsum(lengths) - lengths
    position = lax.axis_index("dp") * row_count + jnp.arange(row_count, dtype=jnp.int32)
    opening = jnp.any(position[:, None] == starts[None, :], axis=1)
    keep = (1.0 - opening.astype(jnp.float32))[:, None]
    table_f = mixer[6].astype(jnp.float32)
    soft = jax.nn.softmax(table_f, axis=0)
    bound = jnp.sum(soft[1 : LAYER + 1], axis=0)
    attn_g = mixer[4].astype(jnp.float32)
    mix_g = mixer[5].astype(jnp.float32)
    mlp_g = dense[3].astype(jnp.float32)
    tokens_wide = whole.astype(jnp.float32)
    inv_tokens = inverse_rms(tokens_wide)
    tokens_hat = tokens_wide * inv_tokens
    normed = (tokens_hat * attn_g).astype(jnp.bfloat16)
    inner = jnp.dot(normed, mixer[0], preferred_element_type=jnp.float32)
    forget_raw = jnp.dot(normed, mixer[1], preferred_element_type=jnp.float32)
    gate_raw = jnp.dot(normed, mixer[2], preferred_element_type=jnp.float32)
    sig_forget = jax.nn.sigmoid(forget_raw)
    forget = bound + (1.0 - bound) * sig_forget
    sig_inner = jax.nn.sigmoid(inner)
    silu_inner = inner * sig_inner
    drive = silu_inner * (1.0 - forget)
    decay = forget * keep
    decay_all, state_all = lax.associative_scan(combine, (decay, drive), axis=0)
    ones_vec = jnp.ones((width,), jnp.float32)
    zeros_vec = jnp.zeros((width,), jnp.float32)
    carry_in = entering(
        (decay_all[-1], state_all[-1]), "dp", combine, (ones_vec, zeros_vec), False
    )[1]
    states = decay_all * carry_in[None, :] + state_all
    inv_states = inverse_rms(states)
    states_hat = states * inv_states
    sig_gate = jax.nn.sigmoid(gate_raw)
    silu_gate = gate_raw * sig_gate
    mixed_in = (states_hat * mix_g * silu_gate).astype(jnp.bfloat16)
    resid = tokens_wide + jnp.dot(mixed_in, mixer[3], preferred_element_type=jnp.float32)
    inv_resid = inverse_rms(resid)
    resid_hat = resid * inv_resid
    hidden_in = (resid_hat * mlp_g).astype(jnp.bfloat16)
    gate_ff = jnp.dot(hidden_in, dense[0], preferred_element_type=jnp.float32)
    up_ff = jnp.dot(hidden_in, dense[1], preferred_element_type=jnp.float32)
    sig_ff = jax.nn.sigmoid(gate_ff)
    silu_ff = gate_ff * sig_ff
    act = (silu_ff * up_ff).astype(jnp.bfloat16)
    partial_out = jnp.dot(act, dense[2], preferred_element_type=jnp.float32)
    glu_out = lax.psum_scatter(
        partial_out.astype(jnp.bfloat16), "mp", scatter_dimension=0, tiled=True
    ).astype(jnp.float32)
    own_resid = lax.dynamic_slice_in_dim(resid, mp_index * half_rows, half_rows, 0)
    result = (own_resid + glu_out).astype(jnp.bfloat16)
    grad_whole = lax.all_gather(out_grad, "mp", axis=0, tiled=True)
    grad_wide = grad_whole.astype(jnp.float32)
    d_act = times_transposed(grad_whole, dense[2])
    grad_down = contract_rows(act, grad_whole)
    d_gate_ff = (d_act * up_ff * sigmoid_slope(gate_ff, sig_ff)).astype(jnp.bfloat16)
    d_up_ff = (d_act * silu_ff).astype(jnp.bfloat16)
    grad_gate_ff = contract_rows(hidden_in, d_gate_ff)
    grad_up_ff = contract_rows(hidden_in, d_up_ff)
    d_hidden_part = times_transposed(d_gate_ff, dense[0]) + times_transposed(d_up_ff, dense[1])
    d_hidden = lax.psum(d_hidden_part, "mp")
    grad_mlp = jnp.sum(d_hidden * resid_hat, axis=0)
    glu_grads = (
        lax.psum_scatter(grad_gate_ff, "dp", scatter_dimension=0, tiled=True),
        lax.psum_scatter(grad_up_ff, "dp", scatter_dimension=0, tiled=True),
        lax.psum_scatter(grad_down, "dp", scatter_dimension=1, tiled=True),
        lax.psum_scatter(grad_mlp, "dp", scatter_dimension=0, tiled=True),
    )
    scaled_hidden = d_hidden * mlp_g
    d_resid = grad_wide + inv_resid * (
        scaled_hidden - resid_hat * jnp.mean(scaled_hidden * resid_hat, axis=-1, keepdims=True)
    )
    d_mixed = d_resid.astype(jnp.bfloat16)
    grad_out = contract_rows(mixed_in, d_mixed)
    d_mixin = times_transposed(d_mixed, mixer[3])
    grad_mix = jnp.sum(d_mixin * states_hat * silu_gate, axis=0)
    d_gate_raw = (d_mixin * states_hat * mix_g * sigmoid_slope(gate_raw, sig_gate)).astype(
        jnp.bfloat16
    )
    scaled_states = d_mixin * mix_g * silu_gate
    d_states = inv_states * (
        scaled_states - states_hat * jnp.mean(scaled_states * states_hat, axis=-1, keepdims=True)
    )
    decay_next = jnp.concatenate([decay[1:], jnp.ones((1, width), jnp.float32)], axis=0)
    tail_all, adjoint_local = lax.associative_scan(
        combine, (decay_next, d_states), reverse=True, axis=0
    )
    first_decay = decay[0]
    incoming = entering(
        (first_decay * tail_all[0], first_decay * adjoint_local[0]),
        "dp",
        combine,
        (ones_vec, zeros_vec),
        True,
    )[1]
    adjoint = adjoint_local + tail_all * incoming[None, :]
    prev_states = jnp.concatenate([carry_in[None, :], states[:-1]], axis=0)
    d_forget = adjoint * prev_states * keep - adjoint * silu_inner
    d_inner = (adjoint * (1.0 - forget) * sigmoid_slope(inner, sig_inner)).astype(jnp.bfloat16)
    d_forget_raw = (d_forget * (1.0 - bound) * sig_forget * (1.0 - sig_forget)).astype(jnp.bfloat16)
    d_bound = jnp.sum(d_forget * (1.0 - sig_forget), axis=0)
    row_ids = jnp.arange(layer_rows)[:, None]
    member = jnp.logical_and(row_ids >= 1, row_ids <= LAYER).astype(jnp.float32)
    grad_table = soft * (member - bound[None, :]) * d_bound[None, :]
    grad_in = contract_rows(normed, d_inner)
    grad_forget = contract_rows(normed, d_forget_raw)
    grad_gate = contract_rows(normed, d_gate_raw)
    d_normed = (
        times_transposed(d_inner, mixer[0])
        + times_transposed(d_forget_raw, mixer[1])
        + times_transposed(d_gate_raw, mixer[2])
    )
    grad_attn = jnp.sum(d_normed * tokens_hat, axis=0)
    scaled_normed = d_normed * attn_g
    d_tokens = d_resid + inv_tokens * (
        scaled_normed - tokens_hat * jnp.mean(scaled_normed * tokens_hat, axis=-1, keepdims=True)
    )
    token_grad = lax.dynamic_slice_in_dim(d_tokens, mp_index * half_rows, half_rows, 0)
    mixer_grads = (
        lax.psum_scatter(grad_in, "dp", scatter_dimension=0, tiled=True),
        lax.psum_scatter(grad_forget, "dp", scatter_dimension=0, tiled=True),
        lax.psum_scatter(grad_gate, "dp", scatter_dimension=0, tiled=True),
        lax.psum_scatter(grad_out, "dp", scatter_dimension=0, tiled=True),
        lax.psum_scatter(grad_attn, "dp", scatter_dimension=0, tiled=True),
        lax.psum_scatter(grad_mix, "dp", scatter_dimension=0, tiled=True),
        lax.psum_scatter(grad_table, "dp", scatter_dimension=1, tiled=True),
    )
    return (
        result,
        token_grad,
        mixer_grads[0],
        mixer_grads[1],
        mixer_grads[2],
        mixer_grads[3],
        mixer_grads[4],
        mixer_grads[5],
        mixer_grads[6],
        glu_grads[0],
        glu_grads[1],
        glu_grads[2],
        glu_grads[3],
    )


def solution(mesh):
    return jax.shard_map(
        per_device,
        mesh=mesh,
        in_specs=(
            P(("dp", "mp"), None),
            P(),
            P("dp", None),
            P("dp", None),
            P("dp", None),
            P("dp", None),
            P("dp"),
            P("dp"),
            P(None, "dp"),
            P("dp", "mp"),
            P("dp", "mp"),
            P("mp", "dp"),
            P("dp"),
            P(("dp", "mp"), None),
        ),
        out_specs=(
            P(("dp", "mp"), None),
            P(("dp", "mp"), None),
            P("dp", None),
            P("dp", None),
            P("dp", None),
            P("dp", None),
            P("dp"),
            P("dp"),
            P(None, "dp"),
            P("dp", "mp"),
            P("dp", "mp"),
            P("mp", "dp"),
            P("dp"),
        ),
        check_vma=False,
    )
```

profile of v0, /device:TPU:0, one launch (start us, length us, event | category | flops | bytes accessed | tf_op | source)
XLA Modules:
  0.0 2432.1 jit_solution(4686550156488616628)
XLA Ops:
  11.9 10.2 all_gather.53
  22.3 22.1 all-gather
  44.5 18.7 all_gather.54
  66.2 18.7 all-gather.3
  85.5 17.7 all-gather.4
  103.8 10.7 all_gather.67
  114.5 4.7 fusion.41
  119.3 44.6 %all-gather.15.cloned.1.call-done = bf16[2048,2048]{1,0:T(8,128)(2,1)} async-done(((bf16[128,2048]{1,0:T(8,128)(2,1)}), bf16[2048,2048]{1,0:T(8,128)(2,1)}) %all-gather.15.cloned.1.call-update) | async-done | bytes 8388624 | tf_op jit(solution)/shard_map/all_gather | solution.py:70
  163.9 6.4 fusion.9
  172.1 3.3 slice.477
  217.3 3.3 slice.507
  241.0 19.5 all-gather.2
  262.4 4.6 pad.186
  270.6 18.3 all-gather.1
  292.4 6.0 multiply_convert_fusion.7
  298.4 17.0 all-gather.21.cloned.1.call-done
  315.4 4.8 multiply_reduce_fusion.7
  320.3 90.0 %all-gather.23.cloned.1.call-done = bf16[2048,2816]{1,0:T(8,128)(2,1)} async-done(((bf16[128,2816]{1,0:T(8,128)(2,1)}), bf16[2048,2816]{1,0:T(8,128)(2,1)}) %all-gather.23.cloned.1.call-update) | async-done | bytes 11534352 | tf_op jit(solution)/shard_map/all_gather | solution.py:78
  410.4 7.1 fusion.58
  417.4 87.6 %all-gather.25.cloned.1.call-done = bf16[2048,2816]{1,0:T(8,128)(2,1)} async-done(((bf16[128,2816]{1,0:T(8,128)(2,1)}), bf16[2048,2816]{1,0:T(8,128)(2,1)}) %all-gather.25.cloned.1.call-update) | async-done | bytes 11534352 | tf_op jit(solution)/shard_map/all_gather | solution.py:79
  505.0 7.0 fusion.59
  512.1 90.7 %all-gather.27.cloned.1.call-done = bf16[2816,2048]{1,0:T(8,128)(2,1)} async-done(((bf16[2816,128]{1,0:T(8,128)(2,1)}), bf16[2816,2048]{1,0:T(8,128)(2,1)}) %all-gather.27.cloned.1.call-update) | async-done | bytes 11534352 | tf_op jit(solution)/shard_map/all_gather | solution.py:80
  602.8 10.3 multiply_convert_fusion
  613.9 8.2 fusion.60
  622.2 4.9 convolution_add_fusion
  630.1 3.3 slice.513
  640.0 8.3 slice.514
  648.2 8.3 slice.521
  656.5 8.3 slice.512
  664.8 7.0 convolution_convert_fusion
  676.7 8.3 multiply_reduce_fusion.2
  692.9 8.2 slice.516
  701.1 8.2 slice.518
  820.6 4.6 pad.229
  832.6 4.6 pad.215
  837.2 8.3 slice.566
  849.1 4.6 pad.214
  855.6 4.6 pad.228
  867.1 19.5 all-gather.5
  886.6 4.8 rev.16
  891.5 18.4 all-gather.6
  909.9 4.8 rev.17
  914.8 13.9 while.29
  928.7 8.9 rev.15
  937.6 8.9 rev.14
  946.4 4.3 multiply_reduce_fusion.1
  954.0 9.0 fusion.38
  964.0 8.4 fusion.39
  973.6 9.2 fusion.15
  982.9 9.2 fusion.37
  992.4 10.6 fusion.62
  1003.0 10.5 fusion.63
  1014.5 14.7 fusion.64
  1031.2 7.9 fusion.61
  1039.1 6.5 convolution_add_fusion.2
  1045.7 4.2 multiply_reduce_fusion.3
  1049.9 62.9 %all-reduce.61 = (f32[2048]{0:T(1024)S(1)}, f32[2048]{0:T(1024)S(1)}, f32[2048]{0:T(1024)S(1)}) all-reduce(f32[2048]{0:T(1024)S(1)} %get-tuple-element.243, f32[2048]{0:T(1024)S(1)} %copy-done.36, f32[2048]{0:T(1024)S(1)} %copy-done.28), channel_id=7, replica_groups=mesh['dp'=16,'mp'=2] {'dp'}, use_global_device_ids=true, to_apply=%region_22.23.clone | all-reduce | flops 6144 | bytes 49152
  1118.5 68.8 %reduce-scatter.14.cloned.1.call-done = f32[128,2048]{1,0:T(8,128)} async-done(((f32[2048,2048]{1,0:T(8,128)}), f32[128,2048]{1,0:T(8,128)}) %reduce-scatter.14.cloned.1.call-update) | async-done | bytes 1048592 | tf_op jit(solution)/shard_map/reduce_scatter | solution.py:207
  1187.3 182.2 %reduce-scatter.12.cloned.1.call-done = f32[128,2048]{1,0:T(8,128)} async-done(((f32[2048,2048]{1,0:T(8,128)}), f32[128,2048]{1,0:T(8,128)}) %reduce-scatter.12.cloned.1.call-update) | async-done | bytes 1048592 | tf_op jit(solution)/shard_map/reduce_scatter | solution.py:206
  1369.4 182.3 %reduce-scatter.18.cloned.1.call-done = f32[128,2048]{1,0:T(8,128)} async-done(((f32[2048,2048]{1,0:T(8,128)}), f32[128,2048]{1,0:T(8,128)}) %reduce-scatter.18.cloned.1.call-update) | async-done | bytes 1048592 | tf_op jit(solution)/shard_map/reduce_scatter | solution.py:209
  1551.7 182.1 %reduce-scatter.16.cloned.1.call-done = f32[128,2048]{1,0:T(8,128)} async-done(((f32[2048,2048]{1,0:T(8,128)}), f32[128,2048]{1,0:T(8,128)}) %reduce-scatter.16.cloned.1.call-update) | async-done | bytes 1048592 | tf_op jit(solution)/shard_map/reduce_scatter | solution.py:208
  1733.9 230.4 %reduce-scatter.22.cloned.1.call-done = f32[128,2816]{1,0:T(8,128)} async-done(((f32[2048,2816]{1,0:T(8,128)}), f32[128,2816]{1,0:T(8,128)}) %reduce-scatter.22.cloned.1.call-update) | async-done | bytes 1441808 | tf_op jit(solution)/shard_map/reduce_scatter | solution.py:150
  1964.3 230.5 %reduce-scatter.24.cloned.1.call-done = f32[128,2816]{1,0:T(8,128)} async-done(((f32[2048,2816]{1,0:T(8,128)}), f32[128,2816]{1,0:T(8,128)}) %reduce-scatter.24.cloned.1.call-update) | async-done | bytes 1441808 | tf_op jit(solution)/shard_map/reduce_scatter | solution.py:151
  2194.8 230.5 %reduce-scatter.26.cloned.1.call-done = f32[2816,128]{1,0:T(8,128)} async-done(((f32[2816,2048]{1,0:T(8,128)}), f32[2816,128]{1,0:T(8,128)}) %reduce-scatter.26.cloned.1.call-update) | async-done | bytes 1441808 | tf_op jit(solution)/shard_map/reduce_scatter | solution.py:152
  (441 shorter events, 263.7 us)
Async XLA Ops:
  7.2 107.3 %all-gather.17.cloned.1.call-start = ((), (), s32[]{:S(2)}) async-start(), calls=%async_computation.10 | async-start | bytes 8912896 | tf_op jit(solution)/shard_map/all_gather | solution.py:69
  7.9 156.0 %all-gather.15.cloned.1.call-start = ((), (), s32[]{:S(2)}) async-start(), calls=%async_computation.9 | async-start | bytes 8912896 | tf_op jit(solution)/shard_map/all_gather | solution.py:70
  8.7 283.7 %all-gather.19.cloned.1.call-start = ((), (), s32[]{:S(2)}) async-start(), calls=%async_computation.11 | async-start | bytes 8912896 | tf_op jit(solution)/shard_map/all_gather | solution.py:71
  9.4 306.0 %all-gather.21.cloned.1.call-start = ((), (), s32[]{:S(2)}) async-start(), calls=%async_computation.12 | async-start | bytes 8912896 | tf_op jit(solution)/shard_map/all_gather | solution.py:72
  10.0 400.4 %all-gather.23.cloned.1.call-start = ((), (), s32[]{:S(2)}) async-start(), calls=%async_computation.13 | async-start | bytes 12255232 | tf_op jit(solution)/shard_map/all_gather | solution.py:78
  10.6 494.5 %all-gather.25.cloned.1.call-start = ((), (), s32[]{:S(2)}) async-start(), calls=%async_computation.14 | async-start | bytes 12255232 | tf_op jit(solution)/shard_map/all_gather | solution.py:79
  11.1 591.6 %all-gather.27.cloned.1.call-start = ((), (), s32[]{:S(2)}) async-start(), calls=%async_computation.15 | async-start | bytes 12255232 | tf_op jit(solution)/shard_map/all_gather | solution.py:80
  11.9 660.0 %all-reduce.64.cloned.1.call-start = ((), (), s32[]{:S(2)}) async-start(), calls=%async_computation.17 | async-start | bytes 2097152 | tf_op jit(solution)/shard_map/psum | solution.py:147
  22.3 141.6 %copy-start.25 = (f32[128]{0:T(128)}, f32[128]{0:T(128)S(1)}, u32[]{:S(2)}) copy-start(f32[128]{0:T(128)S(1)} %add_rsqrt_fusion.2) | copy-start | bytes 1540
  63.3 0.6 copy-start.20
  63.9 0.6 copy-start.24
  64.5 99.4 %copy-start.18 = (f32[2048]{0:T(1024)}, f32[2048]{0:T(1024)S(1)}, u32[]{:S(2)}) copy-start(f32[2048]{0:T(1024)S(1)} %slice_reduce_fusion) | copy-start | bytes 24580
  64.5 99.4 %copy-start.22 = (f32[2048]{0:T(1024)}, f32[2048]{0:T(1024)S(1)}, u32[]{:S(2)}) copy-start(f32[2048]{0:T(1024)S(1)} %broadcast_subtract_fusion) | copy-start | bytes 24580
  66.2 97.7 %copy-start.37 = (f32[128]{0:T(128)}, f32[128]{0:T(128)S(1)}, u32[]{:S(2)}) copy-start(f32[128]{0:T(128)S(1)} %convert_subtract_fusion) | copy-start | bytes 1540
  119.3 51.0 %copy-start.10 = (f32[128,2048]{1,0:T(8,128)}, f32[128,2048]{1,0:T(8,128)S(1)}, u32[]{:S(2)}) copy-start(f32[128,2048]{1,0:T(8,128)S(1)} %fusion.41) | copy-start | bytes 3145732
  170.3 51.7 %copy-start = (f32[128,2048]{1,0:T(8,128)}, f32[128,2048]{1,0:T(8,128)S(1)}, u32[]{:S(2)}) copy-start(f32[128,2048]{1,0:T(8,128)S(1)} %get-tuple-element.282) | copy-start | bytes 3145732
  213.5 17.0 copy-start.35
  215.1 15.7 copy-start.16
  215.7 15.2 copy-start.32
  230.8 6.3 copy-start.31
  231.0 29.5 %copy-start.30 = (f32[1,2048]{1,0:T(1,128)S(1)}, f32[1,2048]{1,0:T(1,128)}, u32[]{:S(2)}) copy-start(f32[1,2048]{1,0:T(1,128)} %slice.583) | copy-start | bytes 24580
  234.9 57.5 %copy-start.26 = (f32[128]{0:T(128)S(1)}, f32[128]{0:T(128)}, u32[]{:S(2)}) copy-start(f32[128]{0:T(128)} %copy-done.25) | copy-start | bytes 1540
  234.9 57.5 %copy-start.29 = (f32[16,1,128]{2,1,0:T(1,128)S(1)}, f32[16,1,128]{2,1,0:T(1,128)}, u32[]{:S(2)}) copy-start(f32[16,1,128]{2,1,0:T(1,128)} %convert_element_type.94) | copy-start | bytes 24580
  237.1 53.0 %copy-start.8 = (f32[128,2048]{1,0:T(8,128)S(1)}, f32[128,2048]{1,0:T(8,128)}, u32[]{:S(2)}) copy-start(f32[128,2048]{1,0:T(8,128)} %pad.201) | copy-start | bytes 3145732
  240.0 50.1 %copy-start.9 = (f32[128,2048]{1,0:T(8,128)}, f32[128,2048]{1,0:T(8,128)S(1)}, u32[]{:S(2)}) copy-start(f32[128,2048]{1,0:T(8,128)S(1)} %pad.200) | copy-start | bytes 3145732
  298.4 21.8 copy-start.11
  298.4 21.8 copy-start.17
  602.8 19.4 slice-start
  602.8 19.4 slice-start.1
  613.1 0.9 copy-start.13
  613.1 9.1 copy-start.12
  613.9 8.2 slice-start.2
  627.2 487.4 %reduce-scatter.10.cloned.1.call-start = ((), (), s32[]{:S(2)}) async-start(), calls=%async_computation.16 | async-start | bytes 786432 | tf_op jit(solution)/shard_map/reduce_scatter | solution.py:133
  671.8 446.7 %reduce-scatter.20.cloned.1.call-start = ((), (), s32[]{:S(2)}) async-start(), calls=%async_computation.22 | async-start | bytes 208896 | tf_op jit(solution)/shard_map/reduce_scatter | solution.py:212
  675.7 1.0 copy-start.1
  675.7 9.2 copy-start.15
  777.4 36.8 %copy-start.34 = (f32[1,2048]{1,0:T(1,128)S(1)}, f32[1,2048]{1,0:T(1,128)}, u32[]{:S(2)}) copy-start(f32[1,2048]{1,0:T(1,128)} %slice.653) | copy-start | bytes 24580
  777.4 47.8 %copy-start.33 = (f32[1,2048]{1,0:T(1,128)S(1)}, f32[1,2048]{1,0:T(1,128)}, u32[]{:S(2)}) copy-start(f32[1,2048]{1,0:T(1,128)} %slice.631) | copy-start | bytes 24580
  849.1 97.3 %copy-start.19 = (f32[2048]{0:T(1024)S(1)}, f32[2048]{0:T(1024)}, u32[]{:S(2)}) copy-start(f32[2048]{0:T(1024)} %copy-done.18) | copy-start | bytes 24580
  849.1 97.3 %copy-start.23 = (f32[2048]{0:T(1024)S(1)}, f32[2048]{0:T(1024)}, u32[]{:S(2)}) copy-start(f32[2048]{0:T(1024)} %copy-done.22) | copy-start | bytes 24580
  862.9 87.8 %copy-start.21 = (f32[2048]{0:T(1024)S(1)}, f32[2048]{0:T(1024)}, u32[]{:S(2)}) copy-start(f32[2048]{0:T(1024)} %copy-done.20) | copy-start | bytes 24580
  953.9 9.1 copy-start.6
  953.9 233.4 %reduce-scatter.14.cloned.1.call-start = ((), (), s32[]{:S(2)}) async-start(), calls=%async_computation.19 | async-start | bytes 17825792 | tf_op jit(solution)/shard_map/reduce_scatter | solution.py:207
  963.0 1.0 copy-start.4
  963.0 1.0 copy-start.27
  963.0 406.5 %reduce-scatter.12.cloned.1.call-start = ((), (), s32[]{:S(2)}) async-start(), calls=%async_computation.18 | async-start | bytes 17825792 | tf_op jit(solution)/shard_map/reduce_scatter | solution.py:206
  972.4 1.2 copy-start.2
  972.4 579.3 %reduce-scatter.18.cloned.1.call-start = ((), (), s32[]{:S(2)}) async-start(), calls=%async_computation.21 | async-start | bytes 17825792 | tf_op jit(solution)/shard_map/reduce_scatter | solution.py:209
  982.9 751.0 %reduce-scatter.16.cloned.1.call-start = ((), (), s32[]{:S(2)}) async-start(), calls=%async_computation.20 | async-start | bytes 17825792 | tf_op jit(solution)/shard_map/reduce_scatter | solution.py:208
  992.2 972.1 %reduce-scatter.22.cloned.1.call-start = ((), (), s32[]{:S(2)}) async-start(), calls=%async_computation.23 | async-start | bytes 24510464 | tf_op jit(solution)/shard_map/reduce_scatter | solution.py:150
  1003.0 1191.9 %reduce-scatter.24.cloned.1.call-start = ((), (), s32[]{:S(2)}) async-start(), calls=%async_computation.24 | async-start | bytes 24510464 | tf_op jit(solution)/shard_map/reduce_scatter | solution.py:151
  1013.5 1.1 copy-start.3
  1013.5 1411.8 %reduce-scatter.26.cloned.1.call-start = ((), (), s32[]{:S(2)}) async-start(), calls=%async_computation.25 | async-start | bytes 24510464 | tf_op jit(solution)/shard_map/reduce_scatter | solution.py:152
  1029.3 0.7 copy-start.38
  1029.3 1.9 copy-start.5
  1031.2 7.9 copy-start.7
  1031.2 14.4 slice-start.3
  1031.2 14.4 copy-start.14
  1039.1 6.5 slice-start.4
  1045.6 4.2 copy-start.28
  1045.7 4.2 copy-start.36
Sparse Core Ops, SparseCore 0:
  10.2 77.9 all-gather.16
  90.3 73.4 all-gather.14
  166.0 73.1 all-gather.18
  241.2 74.0 all-gather.20
  317.5 92.8 all-gather.22
  412.5 92.4 all-gather.24
  507.2 95.5 all-gather.26
  627.3 38.2 all-reduce.63
  671.9 12.7 reduce-scatter.9
  954.0 51.4 reduce-scatter.19
  1010.2 177.0 reduce-scatter.13
  1191.8 177.5 reduce-scatter.11
  1374.1 177.5 reduce-scatter.17
  1556.3 177.5 reduce-scatter.15
  1738.4 225.8 reduce-scatter.21
  1968.8 225.9 reduce-scatter.23
  2199.3 225.9 reduce-scatter.25
where the time goes:
time: 2450 us; the launch traced here: 2430 us
  waiting for transfers between devices  1640 us (67%)
  local copies, waits for them, and re-layouts  276 us (11%)
  blocking collectives  237 us (10%)
  matrix products  165 us (7%)
  other arithmetic  95 us (4%)
    reduce_scatter x1, waiting for transfers between devices, per_device(): lax.psum_scatter(grad_up_ff, 'dp', scatter_dimension=0, tiled=True)  231 us
    reduce_scatter x1, waiting for transfers between devices, per_device(): lax.psum_scatter(grad_down, 'dp', scatter_dimension=1, tiled=True)  231 us
    reduce_scatter x1, waiting for transfers between devices, per_device(): lax.psum_scatter(grad_gate_ff, 'dp', scatter_dimension=0, tiled=True)  230 us
    reduce_scatter x1, waiting for transfers between devices, per_device(): lax.psum_scatter(grad_out, 'dp', scatter_dimension=0, tiled=True)  182 us
    reduce_scatter x1, waiting for transfers between devices, per_device(): lax.psum_scatter(grad_in, 'dp', scatter_dimension=0, tiled=True)  182 us
    reduce_scatter x1, waiting for transfers between devices, per_device(): lax.psum_scatter(grad_gate, 'dp', scatter_dimension=0, tiled=True)  182 us
    slice x49, local copies, waits for them, and re-layouts, per_device(): lax.associative_scan(combine, (decay_next, d_states), reverse=True, axis=0)  121 us
    all_gather x1, waiting for transfers between devices, per_device(): lax.all_gather(ff_down, 'dp', axis=1, tiled=True)  90.7 us
  transfers between devices with their start and end apart: 17, of which 12 were waited for; matrix products, arithmetic and copies ran while one was open for 21% of the time, Pallas kernels for 0%

commit v1 on v0

--- a/solution.py
+++ b/solution.py
@@ -5,6 +5,19 @@
 
 LAYER = 12
 epsilon = 1e-06
+
+
+def gather_around(array, axis, dim):
+    ways = lax.axis_size(axis)
+    up = [(d, (d + 1) % ways) for d in range(ways)]
+    down = [(d, (d - 1) % ways) for d in range(ways)]
+    earlier, later = ([array], [array])
+    for _ in range(ways // 2):
+        earlier.append(lax.ppermute(earlier[-1], axis, up))
+    for _ in range((ways - 1) // 2):
+        later.append(lax.ppermute(later[-1], axis, down))
+    line = jnp.concatenate([*earlier[::-1], *later[1:]], axis=dim)
+    return jnp.roll(line, (lax.axis_index(axis) - ways // 2) * array.shape[dim], axis=dim)
 
 
 def entering(value, axis, join, neutral, backward):
@@ -75,7 +88,7 @@
         lax.all_gather(bound_table, "dp", axis=1, tiled=True),
     )
     dense = (
-        lax.all_gather(ff_gate, "dp", axis=0, tiled=True),
+        gather_around(ff_gate, "dp", 0),
         lax.all_gather(ff_up, "dp", axis=0, tiled=True),
         lax.all_gather(ff_down, "dp", axis=1, tiled=True),
         lax.all_gather(mlp_gain, "dp", axis=0, tiled=True),

time: 2450 us -> 2400 us (0.980)
  waiting for transfers between devices: 1640 us -> 1490 us
  local copies, waits for them, and re-layouts: 276 us -> 318 us
  starting transfers between devices: 0.85 us -> 26.8 us
    all_gather x1 -> x0, waiting for transfers between devices: 90 us -> none  [per_device(): lax.all_gather(ff_gate, 'dp', axis=0, tiled=True)]
    ppermute x0 -> x15, waiting for transfers between devices: none -> 89 us  [the longest x8 86.1 us: gather_around(): earlier.append(lax.ppermute(earlier[-1], axis, up))]
    all_gather x1, waiting for transfers between devices: 87.6 us -> 5.88 us  [per_device(): lax.all_gather(ff_up, 'dp', axis=0, tiled=True)]
    unnamed x96 -> x139, local copies, waits for them, and re-layouts: 9.18 us -> 57 us
    all_gather x1, waiting for transfers between devices: 44.6 us -> 0.02 us  [per_device(): lax.all_gather(w_forget, 'dp', axis=0, tiled=True)]
    ppermute x0 -> x15, starting transfers between devices: none -> 25.9 us  [the longest x7 25.4 us: gather_around(): later.append(lax.ppermute(later[-1], axis, down))]
  transfers between devices with their start and end apart: 17 -> 31, of which waited for: 12 -> 15; matrix products, arithmetic and copies ran while one was open for 21% -> 23% of each run, Pallas kernels for 0% -> 0%
where the time goes in v1:
time: 2400 us; the launch traced here: 2380 us
  waiting for transfers between devices  1490 us (62%)
  local copies, waits for them, and re-layouts  318 us (13%)
  blocking collectives  260 us (11%)
  matrix products  170 us (7%)
  other arithmetic  97.2 us (4%)
  starting transfers between devices  26.8 us (1%)
    reduce_scatter x1, waiting for transfers between devices, per_device(): lax.psum_scatter(grad_down, 'dp', scatter_dimension=1, tiled=True)  231 us
    reduce_scatter x1, waiting for transfers between devices, per_device(): lax.psum_scatter(grad_gate_ff, 'dp', scatter_dimension=0, tiled=True)  230 us
    reduce_scatter x1, waiting for transfers between devices, per_device(): lax.psum_scatter(grad_up_ff, 'dp', scatter_dimension=0, tiled=True)  230 us
    reduce_scatter x1, waiting for transfers between devices, per_device(): lax.psum_scatter(grad_in, 'dp', scatter_dimension=0, tiled=True)  182 us
    reduce_scatter x1, waiting for transfers between devices, per_device(): lax.psum_scatter(grad_gate, 'dp', scatter_dimension=0, tiled=True)  182 us
    reduce_scatter x1, waiting for transfers between devices, per_device(): lax.psum_scatter(grad_out, 'dp', scatter_dimension=0, tiled=True)  182 us
    slice x49, local copies, waits for them, and re-layouts, per_device(): lax.associative_scan(combine, (decay_next, d_states), reverse=True, axis=0)  108 us
    all_gather x1, waiting for transfers between devices, per_device(): lax.all_gather(ff_down, 'dp', axis=1, tiled=True)  90.6 us
  transfers between devices with their start and end apart: 31, of which 15 were waited for; matrix products, arithmetic and copies ran while one was open for 23% of the time, Pallas kernels for 0%

profile of v1, /device:TPU:0, one launch (start us, length us, event | category | flops | bytes accessed | tf_op | source)
XLA Modules:
  0.0 2383.4 jit_solution(7033820559271498536)
XLA Ops:
  11.1 14.3 collective-permute-done
  25.4 4.4 collective-permute-start.8
  29.8 21.5 collective-permute-done.1
  51.4 4.4 collective-permute-start.9
  55.8 23.6 collective-permute-done.2
  84.8 10.9 collective-permute-done.3
  95.7 4.4 collective-permute-start.11
  100.2 15.7 collective-permute-done.4
  115.9 24.5 %all_gather.51 = bf16[24,2048]{1,0:T(8,128)(2,1)S(1)} all-gather(bf16[24,128]{1,0:T(8,128)(2,1)} %param.26), channel_id=1, replica_groups=mesh['dp'=16,'mp'=2] {'dp'}, dimensions={1}, use_global_device_ids=true | all-gather | bytes 104448 | tf_op jit(solution)/shard_map/all_gather | solution.py:88
  144.9 9.3 all_gather.50
  154.2 10.2 all_gather.63
  167.5 4.6 collective-permute-start.13
  172.2 40.4 %all-gather = bf16[16,1,128]{2,1,0:T(2,128)(2,1)S(1)} all-gather(bf16[1,1,128]{2,1,0:T(2,128)(2,1)} %bitcast.100), channel_id=1, replica_groups=mesh['dp'=16,'mp'=2] {'dp'}, dimensions={0}, use_global_device_ids=true | all-gather | bytes 4352 | tf_op jit(solution)/shard_map/all_gather | solution.py:86
  212.7 17.5 all-gather.3
  230.8 18.9 all-gather.4
  302.6 4.8 fusion.50
  307.5 6.7 fusion.16
  411.2 19.6 all-gather.2
  437.7 18.5 all-gather.1
  460.4 6.2 multiply_convert_fusion.7
  466.6 5.0 multiply_reduce_fusion.7
  472.8 5.9 all-gather.22.cloned.1.call-done
  478.7 7.1 fusion.67
  485.7 90.6 %all-gather.24.cloned.1.call-done = bf16[2816,2048]{1,0:T(8,128)(2,1)} async-done(((bf16[2816,128]{1,0:T(8,128)(2,1)}), bf16[2816,2048]{1,0:T(8,128)(2,1)}) %all-gather.24.cloned.1.call-update) | async-done | bytes 11534352 | tf_op jit(solution)/shard_map/all_gather | solution.py:93
  576.3 8.4 fusion.68
  584.7 8.2 multiply_convert_fusion.1
  596.8 9.3 fusion.5
  617.8 8.3 slice.514
  626.1 8.3 slice.521
  634.4 5.1 slice.512
  639.5 7.0 convolution_convert_fusion
  651.4 8.4 multiply_reduce_fusion.2
  667.8 8.3 slice.516
  676.0 5.0 slice.518
  771.2 4.6 pad.229
  783.2 4.6 pad.215
  787.8 8.3 slice.566
  800.4 4.6 pad.214
  806.9 4.6 pad.228
  818.3 19.5 all-gather.5
  837.9 4.8 rev.16
  842.7 18.2 all-gather.6
  861.0 4.8 rev.17
  865.8 13.9 while.29
  879.8 8.9 rev.15
  888.6 8.9 rev.14
  905.0 9.0 fusion.47
  914.1 9.4 fusion.48
  923.6 9.2 fusion.22
  932.9 9.3 fusion.46
  942.5 10.5 fusion.71
  953.0 10.5 fusion.72
  963.7 14.7 fusion.73
  979.8 8.0 fusion.70
  987.8 6.5 convolution_add_fusion.1
  994.4 8.4 multiply_reduce_fusion.3
  1002.7 63.2 %all-reduce.61 = (f32[2048]{0:T(1024)S(1)}, f32[2048]{0:T(1024)S(1)}, f32[2048]{0:T(1024)S(1)}) all-reduce(f32[2048]{0:T(1024)S(1)} %get-tuple-element.243, f32[2048]{0:T(1024)S(1)} %copy-done.44, f32[2048]{0:T(1024)S(1)} %copy-done.40), channel_id=7, replica_groups=mesh['dp'=16,'mp'=2] {'dp'}, use_global_device_ids=true, to_apply=%region_22.23.clone | all-reduce | flops 6144 | bytes 49152
  1071.6 66.7 %reduce-scatter.14.cloned.1.call-done = f32[128,2048]{1,0:T(8,128)} async-done(((f32[2048,2048]{1,0:T(8,128)}), f32[128,2048]{1,0:T(8,128)}) %reduce-scatter.14.cloned.1.call-update) | async-done | bytes 1048592 | tf_op jit(solution)/shard_map/reduce_scatter | solution.py:220
  1138.3 182.3 %reduce-scatter.12.cloned.1.call-done = f32[128,2048]{1,0:T(8,128)} async-done(((f32[2048,2048]{1,0:T(8,128)}), f32[128,2048]{1,0:T(8,128)}) %reduce-scatter.12.cloned.1.call-update) | async-done | bytes 1048592 | tf_op jit(solution)/shard_map/reduce_scatter | solution.py:219
  1320.7 182.2 %reduce-scatter.18.cloned.1.call-done = f32[128,2048]{1,0:T(8,128)} async-done(((f32[2048,2048]{1,0:T(8,128)}), f32[128,2048]{1,0:T(8,128)}) %reduce-scatter.18.cloned.1.call-update) | async-done | bytes 1048592 | tf_op jit(solution)/shard_map/reduce_scatter | solution.py:222
  1502.8 182.3 %reduce-scatter.16.cloned.1.call-done = f32[128,2048]{1,0:T(8,128)} async-done(((f32[2048,2048]{1,0:T(8,128)}), f32[128,2048]{1,0:T(8,128)}) %reduce-scatter.16.cloned.1.call-update) | async-done | bytes 1048592 | tf_op jit(solution)/shard_map/reduce_scatter | solution.py:221
  1685.1 230.4 %reduce-scatter.22.cloned.1.call-done = f32[128,2816]{1,0:T(8,128)} async-done(((f32[2048,2816]{1,0:T(8,128)}), f32[128,2816]{1,0:T(8,128)}) %reduce-scatter.22.cloned.1.call-update) | async-done | bytes 1441808 | tf_op jit(solution)/shard_map/reduce_scatter | solution.py:163
  1915.5 230.4 %reduce-scatter.24.cloned.1.call-done = f32[128,2816]{1,0:T(8,128)} async-done(((f32[2048,2816]{1,0:T(8,128)}), f32[128,2816]{1,0:T(8,128)}) %reduce-scatter.24.cloned.1.call-update) | async-done | bytes 1441808 | tf_op jit(solution)/shard_map/reduce_scatter | solution.py:164
  2145.9 230.6 %reduce-scatter.26.cloned.1.call-done = f32[2816,128]{1,0:T(8,128)} async-done(((f32[2816,2048]{1,0:T(8,128)}), f32[2816,128]{1,0:T(8,128)}) %reduce-scatter.26.cloned.1.call-update) | async-done | bytes 1441808 | tf_op jit(solution)/shard_map/reduce_scatter | solution.py:165
  (511 shorter events, 346.2 us)
Async XLA Ops:
  7.2 283.6 %copy-start.19 = (bf16[128,2816]{1,0:T(8,128)(2,1)S(1)}, bf16[128,2816]{1,0:T(8,128)(2,1)}, u32[]{:S(2)}) copy-start(bf16[128,2816]{1,0:T(8,128)(2,1)} %param.27) | copy-start | bytes 2162692
  7.2 295.4 %all-gather.16.cloned.1.call-start = ((), (), s32[]{:S(2)}) async-start(), calls=%async_computation.10 | async-start | bytes 8912896 | tf_op jit(solution)/shard_map/all_gather | solution.py:82
  7.9 299.5 %all-gather.14.cloned.1.call-start = ((), (), s32[]{:S(2)}) async-start(), calls=%async_computation.9 | async-start | bytes 8912896 | tf_op jit(solution)/shard_map/all_gather | solution.py:83
  8.7 451.7 %all-gather.18.cloned.1.call-start = ((), (), s32[]{:S(2)}) async-start(), calls=%async_computation.11 | async-start | bytes 8912896 | tf_op jit(solution)/shard_map/all_gather | solution.py:84
  9.4 457.2 %all-gather.20.cloned.1.call-start = ((), (), s32[]{:S(2)}) async-start(), calls=%async_computation.12 | async-start | bytes 8912896 | tf_op jit(solution)/shard_map/all_gather | solution.py:85
  10.0 468.7 %all-gather.22.cloned.1.call-start = ((), (), s32[]{:S(2)}) async-start(), calls=%async_computation.13 | async-start | bytes 12255232 | tf_op jit(solution)/shard_map/all_gather | solution.py:92
  10.6 565.8 %all-gather.24.cloned.1.call-start = ((), (), s32[]{:S(2)}) async-start(), calls=%async_computation.14 | async-start | bytes 12255232 | tf_op jit(solution)/shard_map/all_gather | solution.py:93
  10.6 14.8 collective-permute-start
  25.4 26.0 %collective-permute-start.1 = (bf16[128,2816]{1,0:T(8,128)(2,1)S(1)}, bf16[128,2816]{1,0:T(8,128)(2,1)S(1)}, u32[]{:S(2)}, u32[]{:S(2)}) collective-permute-start(bf16[128,2816]{1,0:T(8,128)(2,1)S(1)} %collective-permute-done), channel_id=1, source_target_pairs={{0,2},{2,4},{4,6},{6,8},{8,10},{10,12},{12,14},{14,16},{16,18},{18... | collective-permute-start | bytes 2162696 | tf_op jit(solution)/shard_map/ppermute | solution.py:16
  25.4 26.0 %collective-permute-start.8 = (bf16[128,2816]{1,0:T(8,128)(2,1)}, bf16[128,2816]{1,0:T(8,128)(2,1)S(1)}, u32[]{:S(2)}, u32[]{:S(2)}) collective-permute-start(bf16[128,2816]{1,0:T(8,128)(2,1)} %param.27), channel_id=1, source_target_pairs={{0,30},{2,0},{4,2},{6,4},{8,6},{10,8},{12,10},{14,12},{16,14},{18,... | collective-permute-start | bytes 2162696 | tf_op jit(solution)/shard_map/ppermute | solution.py:18
  51.4 28.1 %collective-permute-start.2 = (bf16[128,2816]{1,0:T(8,128)(2,1)S(1)}, bf16[128,2816]{1,0:T(8,128)(2,1)S(1)}, u32[]{:S(2)}, u32[]{:S(2)}) collective-permute-start(bf16[128,2816]{1,0:T(8,128)(2,1)S(1)} %collective-permute-done.1), channel_id=1, source_target_pairs={{0,2},{2,4},{4,6},{6,8},{8,10},{10,12},{12,14},{14,16},{16,18},{18... | collective-permute-start | bytes 2162696 | tf_op jit(solution)/shard_map/ppermute | solution.py:16
  51.4 28.1 %collective-permute-start.9 = (bf16[128,2816]{1,0:T(8,128)(2,1)S(1)}, bf16[128,2816]{1,0:T(8,128)(2,1)S(1)}, u32[]{:S(2)}, u32[]{:S(2)}) collective-permute-start(bf16[128,2816]{1,0:T(8,128)(2,1)S(1)} %collective-permute-done.8), channel_id=1, source_target_pairs={{0,30},{2,0},{4,2},{6,4},{8,6},{10,8},{12,10},{14,12},{16,14},{18,... | collective-permute-start | bytes 2162696 | tf_op jit(solution)/shard_map/ppermute | solution.py:18
  79.5 16.3 copy-start.22
  79.5 16.2 collective-permute-start.3
  80.4 15.4 collective-permute-start.10
  95.7 20.1 collective-permute-start.4
  95.7 44.8 %collective-permute-start.11 = (bf16[128,2816]{1,0:T(8,128)(2,1)}, bf16[128,2816]{1,0:T(8,128)(2,1)}, u32[]{:S(2)}, u32[]{:S(2)}) collective-permute-start(bf16[128,2816]{1,0:T(8,128)(2,1)} %collective-permute-done.10), channel_id=1, source_target_pairs={{0,30},{2,0},{4,2},{6,4},{8,6},{10,8},{12,10},{14,12},{16,14},{18,... | collective-permute-start | bytes 2162696 | tf_op jit(solution)/shard_map/ppermute | solution.py:18
  115.8 27.4 %collective-permute-start.5 = (bf16[128,2816]{1,0:T(8,128)(2,1)}, bf16[128,2816]{1,0:T(8,128)(2,1)}, u32[]{:S(2)}, u32[]{:S(2)}) collective-permute-start(bf16[128,2816]{1,0:T(8,128)(2,1)} %collective-permute-done.4), channel_id=1, source_target_pairs={{0,2},{2,4},{4,6},{6,8},{8,10},{10,12},{12,14},{14,16},{16,18},{18... | collective-permute-start | bytes 2162696 | tf_op jit(solution)/shard_map/ppermute | solution.py:16
  115.9 530.7 %all-reduce.64.cloned.1.call-start = ((), (), s32[]{:S(2)}) async-start(), calls=%async_computation.16 | async-start | bytes 2097152 | tf_op jit(solution)/shard_map/psum | solution.py:160
  140.6 26.9 %collective-permute-start.12 = (bf16[128,2816]{1,0:T(8,128)(2,1)}, bf16[128,2816]{1,0:T(8,128)(2,1)}, u32[]{:S(2)}, u32[]{:S(2)}) collective-permute-start(bf16[128,2816]{1,0:T(8,128)(2,1)} %collective-permute-done.11), channel_id=1, source_target_pairs={{0,30},{2,0},{4,2},{6,4},{8,6},{10,8},{12,10},{14,12},{16,14},{18,... | collective-permute-start | bytes 2162696 | tf_op jit(solution)/shard_map/ppermute | solution.py:18
  143.2 28.9 %collective-permute-start.6 = (bf16[128,2816]{1,0:T(8,128)(2,1)}, bf16[128,2816]{1,0:T(8,128)(2,1)}, u32[]{:S(2)}, u32[]{:S(2)}) collective-permute-start(bf16[128,2816]{1,0:T(8,128)(2,1)} %collective-permute-done.5), channel_id=1, source_target_pairs={{0,2},{2,4},{4,6},{6,8},{8,10},{10,12},{12,14},{14,16},{16,18},{18... | collective-permute-start | bytes 2162696 | tf_op jit(solution)/shard_map/ppermute | solution.py:16
  144.9 162.6 %copy-start.30 = (f32[2048]{0:T(1024)}, f32[2048]{0:T(1024)S(1)}, u32[]{:S(2)}) copy-start(f32[2048]{0:T(1024)S(1)} %slice_reduce_fusion) | copy-start | bytes 24580
  154.2 312.4 %copy-start = (bf16[128,2048]{1,0:T(8,128)(2,1)}, bf16[128,2048]{1,0:T(8,128)(2,1)S(1)}, u32[]{:S(2)}) copy-start(bf16[128,2048]{1,0:T(8,128)(2,1)S(1)} %all_gather.50) | copy-start | bytes 1572868
  167.5 82.9 %collective-permute-start.13 = (bf16[128,2816]{1,0:T(8,128)(2,1)}, bf16[128,2816]{1,0:T(8,128)(2,1)}, u32[]{:S(2)}, u32[]{:S(2)}) collective-permute-start(bf16[128,2816]{1,0:T(8,128)(2,1)} %collective-permute-done.12), channel_id=1, source_target_pairs={{0,30},{2,0},{4,2},{6,4},{8,6},{10,8},{12,10},{14,12},{16,14},{18,... | collective-permute-start | bytes 2162696 | tf_op jit(solution)/shard_map/ppermute | solution.py:18
  172.1 78.7 %collective-permute-start.7 = (bf16[128,2816]{1,0:T(8,128)(2,1)}, bf16[128,2816]{1,0:T(8,128)(2,1)}, u32[]{:S(2)}, u32[]{:S(2)}) collective-permute-start(bf16[128,2816]{1,0:T(8,128)(2,1)} %collective-permute-done.6), channel_id=1, source_target_pairs={{0,2},{2,4},{4,6},{6,8},{8,10},{10,12},{12,14},{14,16},{16,18},{18... | collective-permute-start | bytes 2162696 | tf_op jit(solution)/shard_map/ppermute | solution.py:16
  250.3 36.8 %copy-start.25 = (bf16[128,2816]{1,0:T(8,128)(2,1)S(1)}, bf16[128,2816]{1,0:T(8,128)(2,1)}, u32[]{:S(2)}) copy-start(bf16[128,2816]{1,0:T(8,128)(2,1)} %copy-done.24) | copy-start | bytes 2162692
  250.3 37.7 %copy-start.23 = (bf16[128,2816]{1,0:T(8,128)(2,1)S(1)}, bf16[128,2816]{1,0:T(8,128)(2,1)}, u32[]{:S(2)}) copy-start(bf16[128,2816]{1,0:T(8,128)(2,1)} %copy-done.22) | copy-start | bytes 2162692
  250.3 42.3 %copy-start.21 = (bf16[128,2816]{1,0:T(8,128)(2,1)S(1)}, bf16[128,2816]{1,0:T(8,128)(2,1)}, u32[]{:S(2)}) copy-start(bf16[128,2816]{1,0:T(8,128)(2,1)} %copy-done.20) | copy-start | bytes 2162692
  250.3 57.1 %copy-start.37 = (f32[128]{0:T(128)}, f32[128]{0:T(128)S(1)}, u32[]{:S(2)}) copy-start(f32[128]{0:T(128)S(1)} %add_rsqrt_fusion.2) | copy-start | bytes 1540
  250.4 57.1 %copy-start.45 = (f32[128]{0:T(128)}, f32[128]{0:T(128)S(1)}, u32[]{:S(2)}) copy-start(f32[128]{0:T(128)S(1)} %convert_subtract_fusion) | copy-start | bytes 1540
  250.4 57.1 %copy-start.34 = (f32[2048]{0:T(1024)}, f32[2048]{0:T(1024)S(1)}, u32[]{:S(2)}) copy-start(f32[2048]{0:T(1024)S(1)} %broadcast_subtract_fusion) | copy-start | bytes 24580
  250.4 27.6 %collective-permute-start.14 = (bf16[128,2816]{1,0:T(8,128)(2,1)}, bf16[128,2816]{1,0:T(8,128)(2,1)S(1)}, u32[]{:S(2)}, u32[]{:S(2)}) collective-permute-start(bf16[128,2816]{1,0:T(8,128)(2,1)} %collective-permute-done.13), channel_id=1, source_target_pairs={{0,30},{2,0},{4,2},{6,4},{8,6},{10,8},{12,10},{14,12},{16,14},{18,... | collective-permute-start | bytes 2162696 | tf_op jit(solution)/shard_map/ppermute | solution.py:18
  307.4 81.8 %copy-start.15 = (f32[128,2048]{1,0:T(8,128)}, f32[128,2048]{1,0:T(8,128)S(1)}, u32[]{:S(2)}) copy-start(f32[128,2048]{1,0:T(8,128)S(1)} %fusion.50) | copy-start | bytes 3145732
  314.2 117.8 %copy-start.9 = (f32[128,2048]{1,0:T(8,128)}, f32[128,2048]{1,0:T(8,128)S(1)}, u32[]{:S(2)}) copy-start(f32[128,2048]{1,0:T(8,128)S(1)} %get-tuple-element.282) | copy-start | bytes 3145732
  388.1 22.0 copy-start.43
  388.1 42.7 %copy-start.42 = (f32[1,2048]{1,0:T(1,128)S(1)}, f32[1,2048]{1,0:T(1,128)}, u32[]{:S(2)}) copy-start(f32[1,2048]{1,0:T(1,128)} %slice.583) | copy-start | bytes 24580
  388.1 72.3 %copy-start.38 = (f32[128]{0:T(128)S(1)}, f32[128]{0:T(128)}, u32[]{:S(2)}) copy-start(f32[128]{0:T(128)} %copy-done.37) | copy-start | bytes 1540
  388.1 72.3 %copy-start.41 = (f32[16,1,128]{2,1,0:T(1,128)S(1)}, f32[16,1,128]{2,1,0:T(1,128)}, u32[]{:S(2)}) copy-start(f32[16,1,128]{2,1,0:T(1,128)} %convert_element_type.94) | copy-start | bytes 24580
  434.7 37.9 %copy-start.29 = (f32[16,1,128]{2,1,0:T(1,128)S(1)}, f32[16,1,128]{2,1,0:T(1,128)}, u32[]{:S(2)}) copy-start(f32[16,1,128]{2,1,0:T(1,128)} %convert_element_type.95) | copy-start | bytes 24580
  436.8 20.9 copy-start.14
  460.3 18.3 copy-start.6
  485.7 107.2 %slice-start = ((s8[11534336]{0:T(1024)(128)(4,1)}), s8[3145728]{0:T(1024)(128)(4,1)S(1)}, s32[]{:S(2)}) async-start(s8[11534336]{0:T(1024)(128)(4,1)} %bitcast.74), calls=%async_computation.25 | async-start | bytes 6291456
  596.8 49.9 %copy-start.3 = (f32[128,2048]{1,0:T(8,128)S(1)}, f32[128,2048]{1,0:T(8,128)}, u32[]{:S(2)}) copy-start(f32[128,2048]{1,0:T(8,128)} %copy-done.2) | copy-start | bytes 3145732
  596.8 52.0 %copy-start.8 = (bf16[128,2048]{1,0:T(8,128)(2,1)S(1)}, bf16[128,2048]{1,0:T(8,128)(2,1)}, u32[]{:S(2)}) copy-start(bf16[128,2048]{1,0:T(8,128)(2,1)} %all_gather.63) | copy-start | bytes 1572868
  596.8 54.6 %copy-start.7 = (f32[128,2048]{1,0:T(8,128)S(1)}, f32[128,2048]{1,0:T(8,128)}, u32[]{:S(2)}) copy-start(f32[128,2048]{1,0:T(8,128)} %copy-done.6) | copy-start | bytes 3145732
  606.2 461.6 %reduce-scatter.10.cloned.1.call-start = ((), (), s32[]{:S(2)}) async-start(), calls=%async_computation.15 | async-start | bytes 786432 | tf_op jit(solution)/shard_map/reduce_scatter | solution.py:146
  646.5 425.1 %reduce-scatter.20.cloned.1.call-start = ((), (), s32[]{:S(2)}) async-start(), calls=%async_computation.21 | async-start | bytes 208896 | tf_op jit(solution)/shard_map/reduce_scatter | solution.py:225
  737.5 159.9 %copy-start.31 = (f32[2048]{0:T(1024)S(1)}, f32[2048]{0:T(1024)}, u32[]{:S(2)}) copy-start(f32[2048]{0:T(1024)} %copy-done.30) | copy-start | bytes 24580
  737.5 159.9 %copy-start.35 = (f32[2048]{0:T(1024)S(1)}, f32[2048]{0:T(1024)}, u32[]{:S(2)}) copy-start(f32[2048]{0:T(1024)} %copy-done.34) | copy-start | bytes 24580
  754.0 147.7 %copy-start.33 = (f32[2048]{0:T(1024)S(1)}, f32[2048]{0:T(1024)}, u32[]{:S(2)}) copy-start(f32[2048]{0:T(1024)} %copy-done.32) | copy-start | bytes 24580
  760.4 144.6 %copy-start.1 = (bf16[128,2048]{1,0:T(8,128)(2,1)S(1)}, bf16[128,2048]{1,0:T(8,128)(2,1)}, u32[]{:S(2)}) copy-start(bf16[128,2048]{1,0:T(8,128)(2,1)} %copy-done) | copy-start | bytes 1572868
  897.5 16.6 copy-start.39
  905.0 233.4 %reduce-scatter.14.cloned.1.call-start = ((), (), s32[]{:S(2)}) async-start(), calls=%async_computation.18 | async-start | bytes 17825792 | tf_op jit(solution)/shard_map/reduce_scatter | solution.py:220
  914.0 406.6 %reduce-scatter.12.cloned.1.call-start = ((), (), s32[]{:S(2)}) async-start(), calls=%async_computation.17 | async-start | bytes 17825792 | tf_op jit(solution)/shard_map/reduce_scatter | solution.py:219
  923.5 579.3 %reduce-scatter.18.cloned.1.call-start = ((), (), s32[]{:S(2)}) async-start(), calls=%async_computation.20 | async-start | bytes 17825792 | tf_op jit(solution)/shard_map/reduce_scatter | solution.py:222
  932.8 752.3 %reduce-scatter.16.cloned.1.call-start = ((), (), s32[]{:S(2)}) async-start(), calls=%async_computation.19 | async-start | bytes 17825792 | tf_op jit(solution)/shard_map/reduce_scatter | solution.py:221
  942.1 973.4 %reduce-scatter.22.cloned.1.call-start = ((), (), s32[]{:S(2)}) async-start(), calls=%async_computation.22 | async-start | bytes 24510464 | tf_op jit(solution)/shard_map/reduce_scatter | solution.py:163
  953.0 1192.9 %reduce-scatter.24.cloned.1.call-start = ((), (), s32[]{:S(2)}) async-start(), calls=%async_computation.23 | async-start | bytes 24510464 | tf_op jit(solution)/shard_map/reduce_scatter | solution.py:164
  963.6 14.8 copy-start.46
  963.6 1412.8 %reduce-scatter.26.cloned.1.call-start = ((), (), s32[]{:S(2)}) async-start(), calls=%async_computation.24 | async-start | bytes 24510464 | tf_op jit(solution)/shard_map/reduce_scatter | solution.py:165
  978.3 16.0 copy-start.28
  978.3 24.4 %copy-start.40 = (f32[2048]{0:T(1024)S(1)}, f32[2048]{0:T(1024)}, u32[]{:S(2)}) copy-start(f32[2048]{0:T(1024)} %get-tuple-element.241) | copy-start | bytes 24580
  978.3 24.4 %copy-start.44 = (f32[2048]{0:T(1024)S(1)}, f32[2048]{0:T(1024)}, u32[]{:S(2)}) copy-start(f32[2048]{0:T(1024)} %get-tuple-element.239) | copy-start | bytes 24580
  978.4 91.1 %copy-start.12 = (f32[128,2048]{1,0:T(8,128)S(1)}, f32[128,2048]{1,0:T(8,128)}, u32[]{:S(2)}) copy-start(f32[128,2048]{1,0:T(8,128)} %copy-done.10) | copy-start | bytes 3145732
  (17 other events, 89.7 us)
Sparse Core Ops, SparseCore 0:
  10.2 114.5 all-gather.15
  127.0 94.1 all-gather.13
  223.4 83.7 all-gather.17
  309.2 73.1 all-gather.19
  384.5 94.1 all-gather.21
  480.7 95.6 all-gather.23
  606.3 38.2 all-reduce.63
  646.9 14.5 reduce-scatter.9
  905.1 51.2 reduce-scatter.19
  960.9 177.3 reduce-scatter.13
  1143.0 177.6 reduce-scatter.11
  1325.2 177.5 reduce-scatter.17
  1507.5 177.5 reduce-scatter.15
  1689.6 225.8 reduce-scatter.21
  1920.0 225.7 reduce-scatter.23
  2150.4 225.9 reduce-scatter.25
